TPU v7x, 256 devices: a whole 4x4x8 slice. The times are simulated.
256 devices in a mesh: dp: 64 (over z, y, core), mp: 4 (over x).
Axes of the slice: x: 4, y: 4, z: 8, core: 2. Of those that a mesh axis runs over, the one named last changes fastest.
Arguments:
- attention: bfloat16 [8192, 2048], P('dp', 'mp'), may hold values from -6 to 6
- residual: bfloat16 [8192, 2048], P('dp', 'mp'), may hold values from -6 to 6
- out_weight: bfloat16 [2048, 2048], P('mp', 'dp'), may hold values from -0.125 to 0.125
- ffn_gain: float32 [2048], P('mp'), may hold values from 0.1 to 1.9
- shared_gate: bfloat16 [2048, 2816], P('dp', 'mp'), may hold values from -0.125 to 0.125
- shared_up: bfloat16 [2048, 2816], P('dp', 'mp'), may hold values from -0.125 to 0.125
- shared_down: bfloat16 [2816, 2048], P('mp', 'dp'), may hold values from -0.109375 to 0.109375
- expert_gate: bfloat16 [64, 2048, 1408], P('dp', None, 'mp'), may hold values from -0.125 to 0.125
- expert_up: bfloat16 [64, 2048, 1408], P('dp', None, 'mp'), may hold values from -0.125 to 0.125
- expert_down: bfloat16 [64, 1408, 2048], P('dp', 'mp'), may hold values from -0.15625 to 0.15625
- route_ids: int32 [8192, 6], P('dp'), may hold values from 0 to 63, all different within a row; in each aligned block of 128 rows (0 to 127, 128 to 255, ...) at most 16 rows name the same one
- route_scores: float32 [8192, 6], P('dp'), may hold values from 0.05 to 1
- placement: int32 [64], replicated, may hold values from 0 to 63, each once
- next_gain: float32 [2048], P('mp'), may hold values from 0.1 to 1.9
Outputs:
- final: bfloat16 [8192, 2048], P('dp', 'mp')
- next_normed: bfloat16 [8192, 2048], P('dp', 'mp')
Inputs may be any that keep to these rules, and one draw needn't show every extreme that they name: `route_ids`: A token's 6 experts differ. In each aligned block of 128 rows (the rows of one index of dp) no expert is named by more than 16 rows, a bound that some block reaches. `placement`: each storage index is used by exactly one expert.
All inputs are finite; a program needn't handle non-finite values.
Results may differ from a plain program's by a relative error of at most 0.0075.
Values may be sent and summed in bfloat16 or wider, within the bound.
A program may use at most 128 MiB of HBM per device.

v0:
```python
import jax
import jax.numpy as jnp
from jax import lax
from jax.sharding import PartitionSpec as P

D = 2048
EPSILON = 1e-06


def matmul(left, right):
    return jnp.dot(left, right, preferred_element_type=jnp.float32)


def local(
    attention,
    residual,
    out_weight,
    ffn_gain,
    shared_gate,
    shared_up,
    shared_down,
    expert_gate,
    expert_up,
    expert_down,
    route_ids,
    route_scores,
    placement,
    next_gain,
):
    tok_rows = attention.shape[0]
    top_count = route_ids.shape[1]
    experts = lax.axis_size("dp")
    capacity = min(tok_rows, 8 * tok_rows // experts)
    model_width = D
    partial_value = matmul(attention, lax.all_gather(out_weight, "dp", axis=1, tiled=True))
    projected = lax.psum_scatter(partial_value, "mp", scatter_dimension=1, tiled=True)
    hidden = (residual.astype(jnp.float32) + projected).astype(jnp.bfloat16)
    hidden_float = hidden.astype(jnp.float32)
    squares = lax.psum(jnp.sum(hidden_float * hidden_float, axis=1), "mp")
    normed = (hidden_float * lax.rsqrt(squares / model_width + EPSILON)[:, None] * ffn_gain).astype(
        jnp.bfloat16
    )
    whole_rows = lax.all_gather(normed, "mp", axis=1, tiled=True)
    flat_ids = route_ids.reshape(-1)
    expert_iota = jnp.arange(experts, dtype=jnp.int32)
    one_hot = (flat_ids[:, None] == expert_iota[None, :]).astype(jnp.int32)
    target = jnp.sum(one_hot * placement[None, :], axis=1)
    slot = jnp.sum((jnp.cumsum(one_hot, axis=0) - one_hot) * one_hot, axis=1)
    dest = target * capacity + slot
    slots = experts * capacity
    hit = (dest[:, None] == jnp.arange(slots, dtype=jnp.int32)[None, :]).reshape(
        tok_rows, top_count, slots
    )
    flat_scores = route_scores.reshape(tok_rows, top_count)
    combine = jnp.sum(jnp.where(hit, flat_scores[:, :, None], 0.0), axis=1)
    pick = jnp.any(hit, axis=1).astype(jnp.bfloat16)
    outgoing = matmul(pick.T, whole_rows).astype(jnp.bfloat16)
    arrived = lax.all_to_all(
        outgoing.reshape(experts, capacity, model_width),
        "dp",
        split_axis=0,
        concat_axis=0,
        tiled=True,
    )
    in_rows = arrived.reshape(slots, model_width)
    gate_val = matmul(in_rows, expert_gate[0])
    up_val = matmul(in_rows, expert_up[0])
    activated = (jax.nn.silu(gate_val) * up_val).astype(jnp.bfloat16)
    partial_out = matmul(activated, expert_down[0]).astype(jnp.bfloat16)
    returned = lax.all_to_all(
        partial_out.reshape(experts, capacity, model_width),
        "dp",
        split_axis=0,
        concat_axis=0,
        tiled=True,
    ).reshape(slots, model_width)
    routed = jnp.dot(
        combine,
        returned.astype(jnp.float32),
        precision=lax.Precision.HIGHEST,
        preferred_element_type=jnp.float32,
    )
    pieces = (
        lax.all_gather(shared_gate, "dp", axis=0, tiled=True),
        lax.all_gather(shared_up, "dp", axis=0, tiled=True),
    )
    shared_gval = matmul(whole_rows, pieces[0])
    shared_uval = matmul(whole_rows, pieces[1])
    shared_act = (jax.nn.silu(shared_gval) * shared_uval).astype(jnp.bfloat16)
    shared_part = matmul(shared_act, lax.all_gather(shared_down, "dp", axis=1, tiled=True))
    mixture = lax.psum_scatter(routed + shared_part, "mp", scatter_dimension=1, tiled=True)
    final = (hidden_float + mixture).astype(jnp.bfloat16)
    final_float = final.astype(jnp.float32)
    final_squares = lax.psum(jnp.sum(final_float * final_float, axis=1), "mp")
    next_normed = (
        final_float * lax.rsqrt(final_squares / model_width + EPSILON)[:, None] * next_gain
    ).astype(jnp.bfloat16)
    return (final, next_normed)


def solution(mesh):
    in_specs = (
        P("dp", "mp"),
        P("dp", "mp"),
        P("mp", "dp"),
        P("mp"),
        P("dp", "mp"),
        P("dp", "mp"),
        P("mp", "dp"),
        P("dp", None, "mp"),
        P("dp", None, "mp"),
        P("dp", "mp", None),
        P("dp", None),
        P("dp", None),
        P(),
        P("mp"),
    )
    out_specs = (P("dp", "mp"), P("dp", "mp"))
    return jax.shard_map(local, mesh=mesh, in_specs=in_specs, out_specs=out_specs, check_vma=False)
```

profile of v0, /device:TPU:8, one launch (start us, length us, event | category | flops | bytes accessed | tf_op | source)
XLA Modules:
  0.0 476.1 jit_solution(9288351023330188056)
XLA Ops:
  7.3 0.7 all-gather.5.cloned.1.call-update
  8.0 82.0 %all-gather.5.cloned.1.call-done = bf16[512,2048]{0,1:T(8,128)(2,1)} async-done(((bf16[512,32]{0,1:T(8,128)(2,1)}), bf16[512,2048]{0,1:T(8,128)(2,1)}) %all-gather.5.cloned.1.call-update) | async-done | bytes 2097168 | tf_op jit(solution)/shard_map/all_gather | solution.py:35
  90.0 3.5 fusion.32
  93.6 0.1 eq.43
  93.9 1.8 reduce-window.6
  95.7 0.3 slice_reduce_fusion
  96.1 0.1 select_reduce_fusion.1
  96.4 0.5 fusion
  96.9 21.4 %reduce-scatter.3.cloned.1.call-done = f32[128,512]{1,0:T(8,128)} async-done(((f32[128,2048]{1,0:T(8,128)}), f32[128,512]{1,0:T(8,128)}) %reduce-scatter.3.cloned.1.call-update) | async-done | bytes 262160 | tf_op jit(solution)/shard_map/reduce_scatter | solution.py:36
  118.4 1.1 fusion.20
  119.5 8.5 %psum.14 = f32[128]{0:T(128)S(1)} all-reduce(f32[128]{0:T(128)S(1)} %get-tuple-element.6), channel_id=1, replica_groups=mesh['dp'=64,'mp'=4] {'mp'}, use_global_device_ids=true, to_apply=%region_8.9 | all-reduce | flops 128 | bytes 1024 | tf_op jit(solution)/shard_map/psum | solution.py:39
  128.1 13.2 %all_gather.16 = bf16[128,2048]{1,0:T(8,128)(2,1)S(1)} all-gather(bf16[128,512]{1,0:T(8,128)(2,1)S(1)} %fusion.22), channel_id=1, replica_groups=mesh['dp'=64,'mp'=4] {'mp'}, dimensions={1}, use_global_device_ids=true | all-gather | bytes 655360 | tf_op jit(solution)/shard_map/all_gather | solution.py:43
  141.3 3.2 convolution_convert_fusion.1
  144.6 10.6 %all-to-all-start = ((bf16[64,16,2048]{2,1,0:T(8,128)(2,1)}), bf16[64,16,2048]{2,1,0:T(8,128)(2,1)}, u32[]{:S(2)}, u32[]{:S(2)}) async-start(bf16[64,16,2048]{2,1,0:T(8,128)(2,1)} %bitcast.50), calls=%async_computation.1 | async-start | bytes 8388608 | tf_op jit(solution)/shard_map/all_to_all | solution.py:58
  155.2 0.7 all-gather.7.cloned.1.call-update
  156.0 0.5 all-gather.11.cloned.1.call-update
  156.5 104.0 %all-to-all-done = bf16[64,16,2048]{2,1,0:T(8,128)(2,1)} async-done(((bf16[64,16,2048]{2,1,0:T(8,128)(2,1)}), bf16[64,16,2048]{2,1,0:T(8,128)(2,1)}, u32[]{:S(2)}, u32[]{:S(2)}) %all-to-all-start) | async-done | bytes 4194336 | tf_op jit(solution)/shard_map/all_to_all | solution.py:58
  260.5 5.1 %fusion.3 = f32[1024,352]{0,1:T(8,128)} fusion(bf16[1024,2048]{1,0:T(8,128)(2,1)} %bitcast.2, bf16[1,2048,352]{1,2,0:T(8,128)(2,1)S(1)} %copy-done.10), kind=kOutput, calls=%fused_computation.9 | convolution fusion | flops 1476395008 | bytes 7077888 | tf_op jit(solution)/shard_map/dot_general | solution.py:11
  265.6 8.9 %convolution_convert_fusion = bf16[1024,2048]{1,0:T(8,128)(2,1)} fusion(bf16[1,352,2048]{2,1,0:T(8,128)(2,1)S(1)} %copy-done, bf16[1024,2048]{1,0:T(8,128)(2,1)} %bitcast.2, bf16[1,2048,352]{1,2,0:T(8,128)(2,1)} %param.22, f32[1024,352]{0,1:T(8,128)} %fusion.3), kind=kOutput, calls=%fused_computation | convolution fusion | flops 2957049856 | bytes 12713984 | tf_op jit(solution)/shard_map/dot_general | solution.py:11
  274.6 5.8 %all-to-all-start.1 = ((bf16[64,16,2048]{2,1,0:T(8,128)(2,1)}), bf16[64,16,2048]{2,1,0:T(8,128)(2,1)}, u32[]{:S(2)}, u32[]{:S(2)}) async-start(bf16[64,16,2048]{2,1,0:T(8,128)(2,1)} %bitcast.51), calls=%async_computation.2 | async-start | bytes 8388608 | tf_op jit(solution)/shard_map/all_to_all | solution.py:70
  280.4 0.5 all-gather.9.cloned.1.call-update
  281.0 0.2 reduce-scatter.5.cloned.1.call-start
  281.2 0.4 select_reduce_fusion
  281.7 3.9 fusion.34
  285.6 98.6 %all-to-all-done.1 = bf16[64,16,2048]{2,1,0:T(8,128)(2,1)} async-done(((bf16[64,16,2048]{2,1,0:T(8,128)(2,1)}), bf16[64,16,2048]{2,1,0:T(8,128)(2,1)}, u32[]{:S(2)}, u32[]{:S(2)}) %all-to-all-start.1) | async-done | bytes 4194336 | tf_op jit(solution)/shard_map/all_to_all | solution.py:70
  384.2 4.0 fusion.33
  388.3 38.4 %all-gather.9.cloned.1.call-done = bf16[2048,704]{1,0:T(8,128)(2,1)} async-done(((bf16[32,704]{1,0:T(8,128)(2,1)}), bf16[2048,704]{1,0:T(8,128)(2,1)}) %all-gather.9.cloned.1.call-update) | async-done | bytes 2883600 | tf_op jit(solution)/shard_map/all_gather | solution.py:85
  426.7 7.3 %convolution_add_fusion = f32[128,2048]{1,0:T(8,128)} fusion(f32[128,2048]{1,0:T(8,128)S(1)} %fusion.33, bf16[704,2048]{0,1:T(8,128)(2,1)} %all-gather.11.cloned.1.call-done, bf16[128,2048]{1,0:T(8,128)(2,1)S(1)} %all_gather.16, bf16[2048,704]{1,0:T(8,128)(2,1)} %all-gather.9.cloned.1.call-done, f32[128,704]{0,1:T(8,128)} %fusion.34), kind=kOutput, calls=%fused_computation.5 | convolution fusion | flops 739000320 | bytes 8749056 | tf_op jit(solution)/shard_map/dot_general | solution.py:11
  434.0 24.9 %reduce-scatter.5.cloned.1.call-done = f32[128,512]{1,0:T(8,128)} async-done(((f32[128,2048]{1,0:T(8,128)}), f32[128,512]{1,0:T(8,128)}) %reduce-scatter.5.cloned.1.call-update) | async-done | bytes 262160 | tf_op jit(solution)/shard_map/reduce_scatter | solution.py:91
  458.9 1.1 fusion.17
  460.0 8.5 %psum.15 = f32[128]{0:T(128)S(1)} all-reduce(f32[128]{0:T(128)S(1)} %get-tuple-element.4), channel_id=1, replica_groups=mesh['dp'=64,'mp'=4] {'mp'}, use_global_device_ids=true, to_apply=%region_11.12 | all-reduce | flops 128 | bytes 1024 | tf_op jit(solution)/shard_map/psum | solution.py:94
  468.5 0.8 fusion.19
  (41 shorter events, 0.9 us)
Async XLA Ops:
  7.2 258.5 %copy-start = (bf16[1,352,2048]{2,1,0:T(8,128)(2,1)S(1)}, bf16[1,352,2048]{2,1,0:T(8,128)(2,1)}, u32[]{:S(2)}) copy-start(bf16[1,352,2048]{2,1,0:T(8,128)(2,1)} %param.23) | copy-start | bytes 4325380
  7.2 86.3 %copy-start.6 = (s32[128,6]{0,1:T(8,128)S(1)}, s32[128,6]{0,1:T(8,128)}, u32[]{:S(2)}) copy-start(s32[128,6]{0,1:T(8,128)} %param.24) | copy-start | bytes 9220
  7.2 88.9 %copy-start.9 = (s32[64]{0:T(128)S(1)}, s32[64]{0:T(128)}, u32[]{:S(2)}) copy-start(s32[64]{0:T(128)} %param.26) | copy-start | bytes 772
  7.2 111.2 %copy-start.4 = (bf16[128,512]{1,0:T(8,128)(2,1)S(1)}, bf16[128,512]{1,0:T(8,128)(2,1)}, u32[]{:S(2)}) copy-start(bf16[128,512]{1,0:T(8,128)(2,1)} %param.15) | copy-start | bytes 393220
  7.2 82.8 %all-gather.5.cloned.1.call-start = ((), (), s32[]{:S(2)}) async-start(), calls=%async_computation.4 | async-start | bytes 2129920 | tf_op jit(solution)/shard_map/all_gather | solution.py:35
  7.9 120.1 %copy-start.7 = (f32[512]{0:T(512)S(1)}, f32[512]{0:T(512)}, u32[]{:S(2)}) copy-start(f32[512]{0:T(512)} %param.17) | copy-start | bytes 6148
  8.0 110.4 %reduce-scatter.3.cloned.1.call-start = ((), (), s32[]{:S(2)}) async-start(), calls=%async_computation.5 | async-start | bytes 1310720 | tf_op jit(solution)/shard_map/reduce_scatter | solution.py:36
  119.5 8.6 %copy-start.1 = (bf16[128,512]{1,0:T(8,128)(2,1)}, bf16[128,512]{1,0:T(8,128)(2,1)S(1)}, u32[]{:S(2)}) copy-start(bf16[128,512]{1,0:T(8,128)(2,1)S(1)} %get-tuple-element.7) | copy-start | bytes 393220
  144.6 116.0 %copy-start.10 = (bf16[1,2048,352]{1,2,0:T(8,128)(2,1)S(1)}, bf16[1,2048,352]{1,2,0:T(8,128)(2,1)}, u32[]{:S(2)}) copy-start(bf16[1,2048,352]{1,2,0:T(8,128)(2,1)} %param.21) | copy-start | bytes 4325380
  144.6 116.0 %all-to-all-start = ((bf16[64,16,2048]{2,1,0:T(8,128)(2,1)}), bf16[64,16,2048]{2,1,0:T(8,128)(2,1)}, u32[]{:S(2)}, u32[]{:S(2)}) async-start(bf16[64,16,2048]{2,1,0:T(8,128)(2,1)} %bitcast.50), calls=%async_computation.1 | async-start | bytes 8388608 | tf_op jit(solution)/shard_map/all_to_all | solution.py:58
  155.2 126.5 %all-gather.7.cloned.1.call-start = ((), (), s32[]{:S(2)}) async-start(), calls=%async_computation.6 | async-start | bytes 3194880 | tf_op jit(solution)/shard_map/all_gather | solution.py:84
  155.9 232.4 %all-gather.11.cloned.1.call-start = ((), (), s32[]{:S(2)}) async-start(), calls=%async_computation.8 | async-start | bytes 3194880 | tf_op jit(solution)/shard_map/all_gather | solution.py:90
  274.6 6.6 %copy-start.5 = (f32[128,6]{0,1:T(8,128)S(1)}, f32[128,6]{0,1:T(8,128)}, u32[]{:S(2)}) copy-start(f32[128,6]{0,1:T(8,128)} %param.25) | copy-start | bytes 9220
  274.6 109.6 %all-to-all-start.1 = ((bf16[64,16,2048]{2,1,0:T(8,128)(2,1)}), bf16[64,16,2048]{2,1,0:T(8,128)(2,1)}, u32[]{:S(2)}, u32[]{:S(2)}) async-start(bf16[64,16,2048]{2,1,0:T(8,128)(2,1)} %bitcast.51), calls=%async_computation.2 | async-start | bytes 8388608 | tf_op jit(solution)/shard_map/all_to_all | solution.py:70
  280.4 146.3 %all-gather.9.cloned.1.call-start = ((), (), s32[]{:S(2)}) async-start(), calls=%async_computation.7 | async-start | bytes 3194880 | tf_op jit(solution)/shard_map/all_gather | solution.py:85
  281.0 177.9 %reduce-scatter.5.cloned.1.call-start = ((), (), s32[]{:S(2)}) async-start(), calls=%async_computation.9 | async-start | bytes 1310720 | tf_op jit(solution)/shard_map/reduce_scatter | solution.py:91
  388.2 70.7 %copy-start.2 = (bf16[128,512]{1,0:T(8,128)(2,1)S(1)}, bf16[128,512]{1,0:T(8,128)(2,1)}, u32[]{:S(2)}) copy-start(bf16[128,512]{1,0:T(8,128)(2,1)} %copy-done.1) | copy-start | bytes 393220
  388.2 80.3 %copy-start.8 = (f32[512]{0:T(512)S(1)}, f32[512]{0:T(512)}, u32[]{:S(2)}) copy-start(f32[512]{0:T(512)} %param.27) | copy-start | bytes 6148
  460.0 9.3 %copy-start.3 = (bf16[128,512]{1,0:T(8,128)(2,1)}, bf16[128,512]{1,0:T(8,128)(2,1)S(1)}, u32[]{:S(2)}) copy-start(bf16[128,512]{1,0:T(8,128)(2,1)S(1)} %get-tuple-element.5) | copy-start | bytes 393220
Sparse Core Ops, SparseCore 0:
  10.8 79.1 all-gather.4
  93.6 24.6 reduce-scatter.2
  159.2 92.0 all-gather.6
  254.3 88.4 all-gather.10
  345.8 80.8 all-gather.8
  434.2 24.7 reduce-scatter.4
where the time goes:
time: 477 us; the launch traced here: 476 us
  waiting for transfers between devices  372 us (78%)
  matrix products  36 us (8%)
  blocking collectives  30.3 us (6%)
  starting transfers between devices  16.8 us (4%)
  between operations  14.3 us (3%)
  other arithmetic  5.93 us (1%)
    all_to_all x1, waiting for transfers between devices, local(): lax.all_to_all(outgoing.reshape(experts, capacity, model_width), 'dp', sp...  104 us
    all_to_all x1, waiting for transfers between devices, local(): lax.all_to_all(partial_out.reshape(experts, capacity, model_width), 'dp',...  98.6 us
    all_gather x1, waiting for transfers between devices, local(): lax.all_gather(out_weight, 'dp', axis=1, tiled=True)  82 us
    all_gather x1, waiting for transfers between devices, local(): lax.all_gather(shared_up, 'dp', axis=0, tiled=True)  38.4 us
    dot_general x6, matrix products, matmul(): return jnp.dot(left, right, preferred_element_type=jnp.float32)  32 us
    reduce_scatter x1, waiting for transfers between devices, local(): lax.psum_scatter(routed + shared_part, 'mp', scatter_dimension=1, tiled=T...  24.9 us
    reduce_scatter x1, waiting for transfers between devices, local(): lax.psum_scatter(partial_value, 'mp', scatter_dimension=1, tiled=True)  21.4 us
    all_gather x1, blocking collectives, local(): whole_rows = lax.all_gather(normed, 'mp', axis=1, tiled=True)  13.2 us
  transfers between devices with their start and end apart: 8, of which 6 were waited for; matrix products, arithmetic and copies ran while one was open for 5% of the time, Pallas kernels for 0%

commit v1 on v0

--- a/solution.py
+++ b/solution.py
@@ -32,7 +32,12 @@
     experts = lax.axis_size("dp")
     capacity = min(tok_rows, 8 * tok_rows // experts)
     model_width = D
-    partial_value = matmul(attention, lax.all_gather(out_weight, "dp", axis=1, tiled=True))
+    partial_value = matmul(
+        attention,
+        jnp.concatenate(
+            lax.all_to_all(jnp.stack([out_weight] * lax.axis_size("dp")), "dp", 0, 0), axis=1
+        ),
+    )
     projected = lax.psum_scatter(partial_value, "mp", scatter_dimension=1, tiled=True)
     hidden = (residual.astype(jnp.float32) + projected).astype(jnp.bfloat16)
     hidden_float = hidden.astype(jnp.float32)

time: 477 us -> 456 us (0.956)
  waiting for transfers between devices: 372 us -> 287 us
  blocking collectives: 30.3 us -> 93.3 us
    all_gather x1 -> x0, waiting for transfers between devices: 82 us -> none  [local(): lax.all_gather(out_weight, 'dp', axis=1, tiled=True)]
    all_to_all x0 -> x1, blocking collectives: none -> 63.2 us  [local(): lax.all_to_all(jnp.stack([out_weight] * lax.axis_size('dp')), 'dp', 0, 0)]
    all_gather x1, waiting for transfers between devices: 0.02 us -> 39.1 us  [local(): lax.all_gather(shared_down, 'dp', axis=1, tiled=True)]
    all_gather x1, waiting for transfers between devices: 38.4 us -> 0.03 us  [local(): lax.all_gather(shared_up, 'dp', axis=0, tiled=True)]
  transfers between devices with their start and end apart: 8 -> 7, of which waited for: 6 -> 5; matrix products, arithmetic and copies ran while one was open for 5% -> 6% of each run, Pallas kernels for 0% -> 0%
where the time goes in v1:
time: 456 us; the launch traced here: 455 us
  waiting for transfers between devices  287 us (63%)
  blocking collectives  93.3 us (20%)
  matrix products  34.3 us (8%)
  starting transfers between devices  16.9 us (4%)
  between operations  15.9 us (3%)
  other arithmetic  5.93 us (1%)
    all_to_all x1, waiting for transfers between devices, local(): lax.all_to_all(outgoing.reshape(experts, capacity, model_width), 'dp', sp...  104 us
    all_to_all x1, waiting for transfers between devices, local(): lax.all_to_all(partial_out.reshape(experts, capacity, model_width), 'dp',...  98.3 us
    all_to_all x1, blocking collectives, local(): lax.all_to_all(jnp.stack([out_weight] * lax.axis_size('dp')), 'dp', 0, 0)  63.2 us
    all_gather x1, waiting for transfers between devices, local(): lax.all_gather(shared_down, 'dp', axis=1, tiled=True)  39.1 us
    dot_general x6, matrix products, matmul(): return jnp.dot(left, right, preferred_element_type=jnp.float32)  30.3 us
    reduce_scatter x1, waiting for transfers between devices, local(): lax.psum_scatter(routed + shared_part, 'mp', scatter_dimension=1, tiled=T...  24.8 us
    reduce_scatter x1, waiting for transfers between devices, local(): lax.psum_scatter(partial_value, 'mp', scatter_dimension=1, tiled=True)  19 us
    all_gather x1, blocking collectives, local(): whole_rows = lax.all_gather(normed, 'mp', axis=1, tiled=True)  13.2 us
  transfers between devices with their start and end apart: 7, of which 5 were waited for; matrix products, arithmetic and copies ran while one was open for 6% of the time, Pallas kernels for 0%

profile of v1, /device:TPU:8, one launch (start us, length us, event | category | flops | bytes accessed | tf_op | source)
XLA Modules:
  0.0 455.4 jit_solution(765891437915690407)
XLA Ops:
  8.1 1.1 stack.2
  9.2 63.2 %all_to_all.15 = bf16[64,512,32]{1,2,0:T(8,128)(2,1)S(1)} all-to-all(bf16[64,512,32]{1,2,0:T(8,128)(2,1)S(1)} %stack.2), channel_id=1, replica_groups=mesh['dp'=64,'mp'=4] {'dp'}, dimensions={0} | all-to-all | bytes 4194304 | tf_op jit(solution)/shard_map/all_to_all | solution.py:38
  72.4 1.8 fusion.32
  74.3 0.1 eq.43
  74.6 1.8 reduce-window.6
  76.4 0.3 slice_reduce_fusion
  76.7 0.1 select_reduce_fusion.1
  77.1 0.5 fusion
  77.6 19.0 %reduce-scatter.3.cloned.1.call-done = f32[128,512]{1,0:T(8,128)} async-done(((f32[128,2048]{1,0:T(8,128)}), f32[128,512]{1,0:T(8,128)}) %reduce-scatter.3.cloned.1.call-update) | async-done | bytes 262160 | tf_op jit(solution)/shard_map/reduce_scatter | solution.py:41
  96.6 1.1 fusion.20
  97.7 8.5 %psum.14 = f32[128]{0:T(128)S(1)} all-reduce(f32[128]{0:T(128)S(1)} %get-tuple-element.6), channel_id=1, replica_groups=mesh['dp'=64,'mp'=4] {'mp'}, use_global_device_ids=true, to_apply=%region_8.9 | all-reduce | flops 128 | bytes 1024 | tf_op jit(solution)/shard_map/psum | solution.py:44
  106.3 13.2 %all_gather.12 = bf16[128,2048]{1,0:T(8,128)(2,1)S(1)} all-gather(bf16[128,512]{1,0:T(8,128)(2,1)S(1)} %fusion.22), channel_id=1, replica_groups=mesh['dp'=64,'mp'=4] {'mp'}, dimensions={1}, use_global_device_ids=true | all-gather | bytes 655360 | tf_op jit(solution)/shard_map/all_gather | solution.py:48
  119.5 3.2 convolution_convert_fusion.1
  122.7 10.7 %all-to-all-start.1 = ((bf16[64,16,2048]{2,1,0:T(8,128)(2,1)}), bf16[64,16,2048]{2,1,0:T(8,128)(2,1)}, u32[]{:S(2)}, u32[]{:S(2)}) async-start(bf16[64,16,2048]{2,1,0:T(8,128)(2,1)} %bitcast.53), calls=%async_computation.2 | async-start | bytes 8388608 | tf_op jit(solution)/shard_map/all_to_all | solution.py:63
  133.5 0.5 all-gather.4.cloned.1.call-update
  134.0 0.5 all-gather.6.cloned.1.call-update
  134.6 104.2 %all-to-all-done.1 = bf16[64,16,2048]{2,1,0:T(8,128)(2,1)} async-done(((bf16[64,16,2048]{2,1,0:T(8,128)(2,1)}), bf16[64,16,2048]{2,1,0:T(8,128)(2,1)}, u32[]{:S(2)}, u32[]{:S(2)}) %all-to-all-start.1) | async-done | bytes 4194336 | tf_op jit(solution)/shard_map/all_to_all | solution.py:63
  238.7 5.1 %fusion.3 = f32[1024,352]{0,1:T(8,128)} fusion(bf16[1024,2048]{1,0:T(8,128)(2,1)} %bitcast.4, bf16[1,2048,352]{1,2,0:T(8,128)(2,1)S(1)} %copy-done.11), kind=kOutput, calls=%fused_computation.9 | convolution fusion | flops 1476395008 | bytes 7077888 | tf_op jit(solution)/shard_map/dot_general | solution.py:11
  243.9 8.9 %convolution_convert_fusion = bf16[1024,2048]{1,0:T(8,128)(2,1)} fusion(bf16[1,352,2048]{2,1,0:T(8,128)(2,1)S(1)} %copy-done, bf16[1024,2048]{1,0:T(8,128)(2,1)} %bitcast.4, bf16[1,2048,352]{1,2,0:T(8,128)(2,1)} %param.22, f32[1024,352]{0,1:T(8,128)} %fusion.3), kind=kOutput, calls=%fused_computation | convolution fusion | flops 2957049856 | bytes 12713984 | tf_op jit(solution)/shard_map/dot_general | solution.py:11
  252.8 5.8 %all-to-all-start.2 = ((bf16[64,16,2048]{2,1,0:T(8,128)(2,1)}), bf16[64,16,2048]{2,1,0:T(8,128)(2,1)}, u32[]{:S(2)}, u32[]{:S(2)}) async-start(bf16[64,16,2048]{2,1,0:T(8,128)(2,1)} %bitcast.55), calls=%async_computation.3 | async-start | bytes 8388608 | tf_op jit(solution)/shard_map/all_to_all | solution.py:75
  258.7 0.5 all-gather.8.cloned.1.call-update
  259.2 0.2 reduce-scatter.5.cloned.1.call-start
  259.4 0.4 select_reduce_fusion
  259.9 3.9 fusion.34
  263.8 98.3 %all-to-all-done.2 = bf16[64,16,2048]{2,1,0:T(8,128)(2,1)} async-done(((bf16[64,16,2048]{2,1,0:T(8,128)(2,1)}), bf16[64,16,2048]{2,1,0:T(8,128)(2,1)}, u32[]{:S(2)}, u32[]{:S(2)}) %all-to-all-start.2) | async-done | bytes 4194336 | tf_op jit(solution)/shard_map/all_to_all | solution.py:75
  362.2 4.0 fusion.33
  366.2 39.1 %all-gather.8.cloned.1.call-done = bf16[704,2048]{0,1:T(8,128)(2,1)} async-done(((bf16[704,32]{0,1:T(8,128)(2,1)}), bf16[704,2048]{0,1:T(8,128)(2,1)}) %all-gather.8.cloned.1.call-update) | async-done | bytes 2883600 | tf_op jit(solution)/shard_map/all_gather | solution.py:95
  405.3 7.3 %convolution_add_fusion = f32[128,2048]{1,0:T(8,128)} fusion(f32[128,2048]{1,0:T(8,128)S(1)} %fusion.33, bf16[704,2048]{0,1:T(8,128)(2,1)} %all-gather.8.cloned.1.call-done, bf16[128,2048]{1,0:T(8,128)(2,1)S(1)} %all_gather.12, bf16[2048,704]{1,0:T(8,128)(2,1)} %all-gather.6.cloned.1.call-done, f32[128,704]{0,1:T(8,128)} %fusion.34), kind=kOutput, calls=%fused_computation.5 | convolution fusion | flops 739000320 | bytes 8749056 | tf_op jit(solution)/shard_map/dot_general | solution.py:11
  412.7 24.8 %reduce-scatter.5.cloned.1.call-done = f32[128,512]{1,0:T(8,128)} async-done(((f32[128,2048]{1,0:T(8,128)}), f32[128,512]{1,0:T(8,128)}) %reduce-scatter.5.cloned.1.call-update) | async-done | bytes 262160 | tf_op jit(solution)/shard_map/reduce_scatter | solution.py:96
  437.5 1.1 fusion.17
  438.5 8.5 %psum.15 = f32[128]{0:T(128)S(1)} all-reduce(f32[128]{0:T(128)S(1)} %get-tuple-element.4), channel_id=1, replica_groups=mesh['dp'=64,'mp'=4] {'mp'}, use_global_device_ids=true, to_apply=%region_11.12 | all-reduce | flops 128 | bytes 1024 | tf_op jit(solution)/shard_map/psum | solution.py:99
  447.0 0.8 fusion.19
  (42 shorter events, 0.9 us)
Async XLA Ops:
  8.0 235.9 %copy-start = (bf16[1,352,2048]{2,1,0:T(8,128)(2,1)S(1)}, bf16[1,352,2048]{2,1,0:T(8,128)(2,1)}, u32[]{:S(2)}) copy-start(bf16[1,352,2048]{2,1,0:T(8,128)(2,1)} %param.23) | copy-start | bytes 4325380
  8.0 64.4 %copy-start.4 = (bf16[128,512]{1,0:T(8,128)(2,1)S(1)}, bf16[128,512]{1,0:T(8,128)(2,1)}, u32[]{:S(2)}) copy-start(bf16[128,512]{1,0:T(8,128)(2,1)} %param.14) | copy-start | bytes 393220
  8.0 88.6 %reduce-scatter.3.cloned.1.call-start = ((), (), s32[]{:S(2)}) async-start(), calls=%async_computation.5 | async-start | bytes 1310720 | tf_op jit(solution)/shard_map/reduce_scatter | solution.py:41
  72.4 1.8 copy-start.7
  72.4 4.4 copy-start.10
  72.4 24.2 %copy-start.5 = (bf16[128,512]{1,0:T(8,128)(2,1)S(1)}, bf16[128,512]{1,0:T(8,128)(2,1)}, u32[]{:S(2)}) copy-start(bf16[128,512]{1,0:T(8,128)(2,1)} %param.15) | copy-start | bytes 393220
  72.4 33.9 %copy-start.8 = (f32[512]{0:T(512)S(1)}, f32[512]{0:T(512)}, u32[]{:S(2)}) copy-start(f32[512]{0:T(512)} %param.17) | copy-start | bytes 6148
  97.7 8.6 %copy-start.1 = (bf16[128,512]{1,0:T(8,128)(2,1)}, bf16[128,512]{1,0:T(8,128)(2,1)S(1)}, u32[]{:S(2)}) copy-start(bf16[128,512]{1,0:T(8,128)(2,1)S(1)} %get-tuple-element.7) | copy-start | bytes 393220
  122.7 116.0 %copy-start.11 = (bf16[1,2048,352]{1,2,0:T(8,128)(2,1)S(1)}, bf16[1,2048,352]{1,2,0:T(8,128)(2,1)}, u32[]{:S(2)}) copy-start(bf16[1,2048,352]{1,2,0:T(8,128)(2,1)} %param.21) | copy-start | bytes 4325380
  122.7 116.0 %all-to-all-start.1 = ((bf16[64,16,2048]{2,1,0:T(8,128)(2,1)}), bf16[64,16,2048]{2,1,0:T(8,128)(2,1)}, u32[]{:S(2)}, u32[]{:S(2)}) async-start(bf16[64,16,2048]{2,1,0:T(8,128)(2,1)} %bitcast.53), calls=%async_computation.2 | async-start | bytes 8388608 | tf_op jit(solution)/shard_map/all_to_all | solution.py:63
  133.4 126.5 %all-gather.4.cloned.1.call-start = ((), (), s32[]{:S(2)}) async-start(), calls=%async_computation.6 | async-start | bytes 3194880 | tf_op jit(solution)/shard_map/all_gather | solution.py:89
  134.0 232.3 %all-gather.6.cloned.1.call-start = ((), (), s32[]{:S(2)}) async-start(), calls=%async_computation.7 | async-start | bytes 3194880 | tf_op jit(solution)/shard_map/all_gather | solution.py:90
  252.8 6.6 %copy-start.6 = (f32[128,6]{0,1:T(8,128)S(1)}, f32[128,6]{0,1:T(8,128)}, u32[]{:S(2)}) copy-start(f32[128,6]{0,1:T(8,128)} %param.25) | copy-start | bytes 9220
  252.8 109.4 %all-to-all-start.2 = ((bf16[64,16,2048]{2,1,0:T(8,128)(2,1)}), bf16[64,16,2048]{2,1,0:T(8,128)(2,1)}, u32[]{:S(2)}, u32[]{:S(2)}) async-start(bf16[64,16,2048]{2,1,0:T(8,128)(2,1)} %bitcast.55), calls=%async_computation.3 | async-start | bytes 8388608 | tf_op jit(solution)/shard_map/all_to_all | solution.py:75
  258.6 146.7 %all-gather.8.cloned.1.call-start = ((), (), s32[]{:S(2)}) async-start(), calls=%async_computation.8 | async-start | bytes 3194880 | tf_op jit(solution)/shard_map/all_gather | solution.py:95
  259.2 178.3 %reduce-scatter.5.cloned.1.call-start = ((), (), s32[]{:S(2)}) async-start(), calls=%async_computation.9 | async-start | bytes 1310720 | tf_op jit(solution)/shard_map/reduce_scatter | solution.py:96
  366.2 71.3 %copy-start.2 = (bf16[128,512]{1,0:T(8,128)(2,1)S(1)}, bf16[128,512]{1,0:T(8,128)(2,1)}, u32[]{:S(2)}) copy-start(bf16[128,512]{1,0:T(8,128)(2,1)} %copy-done.1) | copy-start | bytes 393220
  366.2 80.8 %copy-start.9 = (f32[512]{0:T(512)S(1)}, f32[512]{0:T(512)}, u32[]{:S(2)}) copy-start(f32[512]{0:T(512)} %param.27) | copy-start | bytes 6148
  438.5 9.3 %copy-start.3 = (bf16[128,512]{1,0:T(8,128)(2,1)}, bf16[128,512]{1,0:T(8,128)(2,1)S(1)}, u32[]{:S(2)}) copy-start(bf16[128,512]{1,0:T(8,128)(2,1)S(1)} %get-tuple-element.5) | copy-start | bytes 393220
Sparse Core Ops, SparseCore 0:
  74.3 22.2 reduce-scatter.2
  412.8 24.6 reduce-scatter.4
Sparse Core Ops, SparseCore 1:
  137.0 92.9 all-gather.3
  232.9 87.9 all-gather.5
  323.9 81.4 all-gather.7
